TPU v7x, 128 devices: a whole 4x4x4 slice. The times are simulated.
128 devices in a mesh: row: 64 (over z, y, x), col: 2 (over core).
Axes of the slice: x: 4, y: 4, z: 4, core: 2. Of those that a mesh axis runs over, the one named last changes fastest.
Arguments:
- factor: bfloat16 [2, 8192, 65536], P(None, 'row', 'col'), may hold values from -40 to 40
- scales: float32 [2, 64, 512], P(None, 'row', 'col'), may hold values from 0 to 1, as said below
- coords: float32 [2, 2, 8192], replicated, may hold values from 0 to 1
- jitter: float32 [1], replicated, may hold values from 1 to 2
Outputs:
- new_columns: float32 [2, 8192, 256], P(None, ('row', 'col'))
Inputs may be any that keep to these rules, and one draw needn't show every extreme that they name: `scales`: positive.
All inputs are finite; a program needn't handle non-finite values.
Results may differ from a plain program's by a relative error of at most 0.0003.
Values may be sent and summed in bfloat16 or wider, within the bound.
No kernel may reach another device: no remote copies, remote signals or barrier semaphores. Data moves between devices by JAX's collectives and lax.ppermute only.
A program may use at most 192 MiB of HBM per device.

v0:
```python
import jax
import jax.numpy as jnp
from jax import lax
from jax.sharding import PartitionSpec as P

PANEL = 128


SQRT_THREE = 1.7320508075688772
LENGTH_SCALE = 0.25


def broadcast(value, axis, root):
    mine = lax.axis_index(axis) == root
    return lax.psum(jnp.where(mine, value, jnp.zeros_like(value)), axis)


def matern(left_pts, right_pts):
    diff_x = left_pts[0][:, None] - right_pts[0][None, :]
    diff_y = left_pts[1][:, None] - right_pts[1][None, :]
    scaled = SQRT_THREE * jnp.sqrt(diff_x * diff_x + diff_y * diff_y) / LENGTH_SCALE
    return (1.0 + scaled) * jnp.exp(-scaled)


def right_solve(factor_low, values):
    return jax.scipy.linalg.solve_triangular(factor_low, values.T, lower=True).T


def on_device(factor, scales, coords, jitter):
    cycles, block_rows, width_local = factor.shape
    blocks_local = scales.shape[2]
    lead_width = 2 * PANEL
    widened = (
        factor.astype(jnp.float32).reshape(cycles, block_rows, blocks_local, PANEL)
        * scales[:, :, :, None]
    )
    dequant = widened.astype(jnp.bfloat16).reshape(cycles * block_rows, width_local)
    own_block = dequant[:PANEL]
    rows_one = broadcast(own_block, "row", 0)
    rows_two = broadcast(own_block, "row", 1)
    leading = jnp.concatenate([rows_one, rows_two], axis=0)
    products = lax.dot_general(
        dequant, leading, (((1,), (1,)), ((), ())), preferred_element_type=jnp.float32
    )
    row_index = lax.axis_index("row")
    col_index = lax.axis_index("col")
    row_count = lax.axis_size("row")
    col_count = lax.axis_size("col")
    share_rows = PANEL // col_count
    own_pts = lax.dynamic_slice_in_dim(coords, row_index * PANEL, PANEL, 2).reshape(
        2, cycles * PANEL
    )
    lead_pts = coords[:, 0, :lead_width]
    local_rows = jnp.arange(cycles * PANEL, dtype=jnp.int32)
    global_rows = local_rows // PANEL * (row_count * PANEL) + row_index * PANEL + local_rows % PANEL
    identity_mask = (
        global_rows[:, None] == jnp.arange(lead_width, dtype=jnp.int32)[None, :]
    ).astype(jnp.float32)
    kernel = matern(own_pts, lead_pts) + jitter[0] * identity_mask
    summed = lax.psum(products, "col")
    window = kernel - summed
    block_one = broadcast(jnp.linalg.cholesky(window[:PANEL, :PANEL]), "row", 0)
    cols_one = right_solve(block_one, window[:, :PANEL])
    link_rows = broadcast(cols_one[:PANEL], "row", 1)
    remain = window[:, PANEL:] - jnp.dot(cols_one, link_rows.T, precision=lax.Precision.HIGHEST)
    block_two = broadcast(jnp.linalg.cholesky(remain[:PANEL]), "row", 1)
    cols_two = right_solve(block_two, remain)
    result = jnp.concatenate([cols_one, cols_two], axis=1).reshape(cycles, PANEL, lead_width)
    return lax.dynamic_slice_in_dim(result, col_index * share_rows, share_rows, 1)


def solution(mesh):
    placed = (P(None, "row", "col"), P(None, "row", "col"), P(), P())
    return jax.shard_map(
        on_device,
        mesh=mesh,
        in_specs=placed,
        out_specs=P(None, ("row", "col"), None),
        check_vma=False,
    )
```

profile of v0, /device:TPU:0, one launch (start us, length us, event | category | flops | bytes accessed | tf_op | source)
XLA Modules:
  0.0 726.3 jit_solution(10625960806328132936)
XLA Ops:
  6.5 0.0 all-reduce.15.cloned.1.call-start
  6.5 0.7 copy.23
  7.2 10.0 %copy.16 = f32[32,8,256,128]{3,2,1,0:T(8,128)S(1)} copy(bf16[32,8,256,128]{3,1,2,0:T(8,128)(2,1)} %bitcast.65) | data formatting | bytes 50331648
  17.2 6.2 broadcast_select_fusion.1
  23.4 20.1 %copy_bitcast_fusion = (bf16[128,32768]{1,0:T(8,128)(2,1)}, bf16[128,32768]{1,0:T(8,128)(2,1)}) fusion(bf16[16,8,256,128]{3,2,1,0:T(8,128)(2,1)} %bitcast.67, bf16[16,8,256,128]{3,2,1,0:T(8,128)(2,1)} %bitcast.66), kind=kLoop, calls=%fused_computation.8 | loop fusion | bytes 33554432 | tf_op jit(solution)/shard_map/jit(_where)/select_n | solution.py:15
  43.5 0.0 all-reduce.15.cloned.1.call-update
  43.5 0.0 all-reduce.7.cloned.1.call-start
  43.6 0.7 dynamic-slice_bitcast_fusion.1
  44.3 4.8 mul.58
  49.1 23.0 %fusion = bf16[256,32768]{1,0:T(8,128)(2,1)} fusion(f32[32,8,256,128]{3,2,1,0:T(8,128)S(1)} %bitcast.63, bf16[2,128,32768]{2,1,0:T(8,128)(2,1)} %param.7), kind=kLoop, calls=%fused_computation.1 | loop fusion | flops 25165824 | bytes 67108864 | tf_op jit(solution)/shard_map/convert_element_type | solution.py:37
  72.1 190.9 %all-reduce.15.cloned.1.call-done = (bf16[128,32768]{1,0:T(8,128)(2,1)}, bf16[128,32768]{1,0:T(8,128)(2,1)}) async-done(((bf16[128,32768]{1,0:T(8,128)(2,1)}, bf16[128,32768]{1,0:T(8,128)(2,1)}), (bf16[128,32768]{1,0:T(8,128)(2,1)}, bf16[128,32768]{1,0:T(8,128)(2,1)})) %all-reduce.15.cloned.1.call-update) | async-done | bytes 16777232 | tf_op jit(solution)/shard_map/psum | solution.py:15
  262.9 13.6 %fusion.2 = f32[256,256]{0,1:T(8,128)} fusion(bf16[256,32768]{1,0:T(8,128)(2,1)} %fusion, bf16[128,32768]{1,0:T(8,128)(2,1)} %get-tuple-element.6, bf16[128,32768]{1,0:T(8,128)(2,1)} %get-tuple-element.8), kind=kOutput, calls=%fused_computation.4 | convolution fusion | flops 4328521728 | bytes 33816576 | tf_op jit(solution)/shard_map/dot_general | solution.py:42
  276.5 0.0 all-reduce.7.cloned.1.call-update
  276.5 0.2 all-reduce.9.cloned.1.call-start
  277.4 0.7 fusion.20
  278.1 20.4 %all-reduce.7.cloned.1.call-done = f32[256,256]{0,1:T(8,128)} async-done(((f32[256,256]{0,1:T(8,128)}), f32[256,256]{0,1:T(8,128)}) %all-reduce.7.cloned.1.call-update) | async-done | bytes 262160 | tf_op jit(solution)/shard_map/psum | solution.py:60
  298.5 1.2 add_subtract_fusion
  299.7 0.1 copy.6
  299.8 11.7 %cholesky.44 = f32[128,128]{1,0:T(8,128)S(1)} custom-call(f32[128,128]{1,0:T(8,128)S(1)} %fusion.11), custom_call_target="Cholesky" | custom-call | tf_op jit(solution)/shard_map/jit(cholesky)/cholesky | solution.py:62
  311.6 0.7 compare_reduce_fusion.1
  312.3 1.3 fusion.13
  313.6 0.0 all-reduce.9.cloned.1.call-update
  313.7 0.0 all-reduce.11.cloned.1.call-start
  313.7 124.8 %all-reduce.9.cloned.1.call-done = f32[128,128]{1,0:T(8,128)} async-done(((f32[128,128]{1,0:T(8,128)}), f32[128,128]{1,0:T(8,128)}) %all-reduce.9.cloned.1.call-update) | async-done | bytes 65552 | tf_op jit(solution)/shard_map/psum | solution.py:15
  438.5 0.8 select_bitcast_fusion.1
  439.3 9.8 %custom-call.6 = f32[1,128,128]{1,2,0:T(8,128)S(1)} custom-call(f32[1,128,128]{2,1,0:T(8,128)S(1)} %select_bitcast_fusion.1), custom_call_target="InvertDiagBlocksLowerTriangular" | custom-call | tf_op jit(solution)/shard_map/jit(_solve_triangular)/triangular_solve | solution.py:26
  449.2 0.3 fusion.6
  449.5 0.1 copy.7
  449.6 0.6 slice_select_fusion
  450.2 0.0 all-reduce.11.cloned.1.call-update
  450.2 0.3 all-reduce.13.cloned.1.call-start
  450.5 121.1 %all-reduce.11.cloned.1.call-done = f32[128,128]{1,0:T(8,128)} async-done(((f32[128,128]{1,0:T(8,128)}), f32[128,128]{1,0:T(8,128)}) %all-reduce.11.cloned.1.call-update) | async-done | bytes 65552 | tf_op jit(solution)/shard_map/psum | solution.py:15
  571.6 1.1 convolution_subtract_fusion
  572.7 0.1 copy.9
  572.8 11.7 %cholesky.55 = f32[128,128]{1,0:T(8,128)S(1)} custom-call(f32[128,128]{1,0:T(8,128)S(1)} %fusion.9), custom_call_target="Cholesky" | custom-call | tf_op jit(solution)/shard_map/jit(cholesky)/cholesky | solution.py:66
  584.6 0.7 compare_reduce_fusion
  585.3 1.3 select_select_fusion
  586.6 0.0 all-reduce.13.cloned.1.call-update
  586.6 121.3 %all-reduce.13.cloned.1.call-done = f32[128,128]{1,0:T(8,128)} async-done(((f32[128,128]{1,0:T(8,128)}), f32[128,128]{1,0:T(8,128)}) %all-reduce.13.cloned.1.call-update) | async-done | bytes 65552 | tf_op jit(solution)/shard_map/psum | solution.py:15
  708.0 0.8 select_bitcast_fusion
  708.8 9.8 %custom-call.7 = f32[1,128,128]{1,2,0:T(8,128)S(1)} custom-call(f32[1,128,128]{2,1,0:T(8,128)S(1)} %select_bitcast_fusion), custom_call_target="InvertDiagBlocksLowerTriangular" | custom-call | tf_op jit(solution)/shard_map/jit(_solve_triangular)/triangular_solve | solution.py:26
  718.7 0.4 convolution_bitcast_fusion
  719.1 0.7 constant_dynamic-slice_fusion
  (9 shorter events, 0.1 us)
Async XLA Ops:
  6.5 256.4 %all-reduce.15.cloned.1.call-start = ((), (), s32[]{:S(2)}) async-start(), calls=%async_computation.4 | async-start | bytes 33554432 | tf_op jit(solution)/shard_map/psum | solution.py:15
  43.5 255.0 %all-reduce.7.cloned.1.call-start = ((), (), s32[]{:S(2)}) async-start(), calls=%async_computation | async-start | bytes 524288 | tf_op jit(solution)/shard_map/psum | solution.py:60
  276.5 161.9 %all-reduce.9.cloned.1.call-start = ((), (), s32[]{:S(2)}) async-start(), calls=%async_computation.1 | async-start | bytes 131072 | tf_op jit(solution)/shard_map/psum | solution.py:15
  313.7 257.9 %all-reduce.11.cloned.1.call-start = ((), (), s32[]{:S(2)}) async-start(), calls=%async_computation.2 | async-start | bytes 131072 | tf_op jit(solution)/shard_map/psum | solution.py:15
  450.2 257.8 %all-reduce.13.cloned.1.call-start = ((), (), s32[]{:S(2)}) async-start(), calls=%async_computation.3 | async-start | bytes 131072 | tf_op jit(solution)/shard_map/psum | solution.py:15
Sparse Core Ops, SparseCore 0:
  43.6 219.2 all-reduce.14
  276.7 21.7 all-reduce.6
  313.8 124.6 all-reduce.8
  450.4 121.1 all-reduce.10
  586.8 121.1 all-reduce.12
where the time goes:
time: 727 us; the launch traced here: 726 us
  waiting for transfers between devices  578 us (80%)
  other arithmetic  80 us (11%)
  local copies, waits for them, and re-layouts  37.9 us (5%)
  matrix products  15.4 us (2%)
  between operations  13.9 us (2%)
    psum x4, waiting for transfers between devices, broadcast(): return lax.psum(jnp.where(mine, value, jnp.zeros_like(value)), axis)  558 us
    convert_element_type x1, other arithmetic, on_device(): widened.astype(jnp.bfloat16).reshape(cycles * block_rows, width_local)  23 us
    another operation x4, other arithmetic, right_solve(): return jax.scipy.linalg.solve_triangular(factor_low, values.T, lower=True).T  21.3 us
    psum x1, waiting for transfers between devices, on_device(): summed = lax.psum(products, 'col')  20.4 us
    select_n x1, local copies, waits for them, and re-layouts, broadcast(): return lax.psum(jnp.where(mine, value, jnp.zeros_like(value)), axis)  20.1 us
  transfers between devices with their start and end apart: 5, of which 5 were waited for; matrix products, arithmetic and copies ran while one was open for 4% of the time, Pallas kernels for 0%

commit v1 on v0

v1 whole, which is shorter than its diff:
```python
import jax
import jax.numpy as jnp
from jax import lax
from jax.experimental import pallas as pl
from jax.experimental.pallas import tpu as pltpu
from jax.sharding import PartitionSpec as P

PANEL = 128
LEAD = 2 * PANEL
SQRT_THREE = 1.7320508075688772
LENGTH_SCALE = 0.25
HIGHEST = lax.Precision.HIGHEST
TN = (((1,), (1,)), ((), ()))
TT = (((0,), (0,)), ((), ()))

STEP = 2048
SUB = 32


def vmem():
    return pl.BlockSpec(memory_space=pltpu.VMEM)


def smem():
    return pl.BlockSpec(memory_space=pltpu.SMEM)


def scaled(block, scale_ref, row, first):
    parts = [
        (block[:, j * PANEL : (j + 1) * PANEL].astype(jnp.float32) * scale_ref[row, first + j]).astype(jnp.bfloat16)
        for j in range(block.shape[1] // PANEL)
    ]
    return jnp.concatenate(parts, axis=1)


def dequant_kernel(scale_ref, factor_ref, out_ref):
    first = pl.program_id(0) * (STEP // PANEL)
    out_ref[...] = scaled(factor_ref[0], scale_ref, 0, first)


def dequantize_lead(factor, scales):
    width = factor.shape[2]
    return pl.pallas_call(
        dequant_kernel,
        grid=(width // STEP,),
        in_specs=[smem(), pl.BlockSpec((1, PANEL, STEP), lambda k: (0, 0, k))],
        out_specs=pl.BlockSpec((PANEL, STEP), lambda k: (0, k)),
        out_shape=jax.ShapeDtypeStruct((PANEL, width), jnp.bfloat16),
        name="dequantize_lead",
    )(scales, factor)


def products_kernel(col_ref, scale_ref, factor_ref, one_ref, two_ref, send_ref, keep_ref, acc_ref):
    step = pl.program_id(0)

    @pl.when(step == 0)
    def _():
        acc_ref[...] = jnp.zeros_like(acc_ref)

    first = step * (STEP // PANEL)
    lead = jnp.concatenate([one_ref[...], two_ref[...]], axis=0)
    left = jnp.concatenate(
        [scaled(factor_ref[0], scale_ref, 0, first), scaled(factor_ref[1], scale_ref, 1, first), lead], axis=0
    )
    acc_ref[...] += lax.dot_general(left, lead, TN, preferred_element_type=jnp.float32)

    @pl.when(step == pl.num_programs(0) - 1)
    def _():
        share = PANEL // 2
        mine = col_ref[0] * share
        other = share - mine
        for c in range(2):
            here = pl.ds(c * share, share)
            keep_ref[here, :] = acc_ref[pl.ds(pl.multiple_of(c * PANEL + mine, share), share), :]
            send_ref[here, :] = acc_ref[pl.ds(pl.multiple_of(c * PANEL + other, share), share), :]
        keep_ref[PANEL:, :] = acc_ref[LEAD:, :]
        send_ref[PANEL:, :] = acc_ref[LEAD:, :]


def partial_products(col_index, factor, scales, one, two):
    width = factor.shape[2]
    out = jax.ShapeDtypeStruct((PANEL + LEAD, LEAD), jnp.float32)
    return pl.pallas_call(
        products_kernel,
        grid=(width // STEP,),
        in_specs=[
            smem(),
            smem(),
            pl.BlockSpec((2, PANEL, STEP), lambda k: (0, 0, k)),
            pl.BlockSpec((PANEL, STEP), lambda k: (0, k)),
            pl.BlockSpec((PANEL, STEP), lambda k: (0, k)),
        ],
        out_specs=[pl.BlockSpec((PANEL + LEAD, LEAD), lambda k: (0, 0))] * 2,
        out_shape=[out, out],
        scratch_shapes=[pltpu.VMEM((2 * LEAD, LEAD), jnp.float32)],
        name="partial_products",
    )(col_index, scales, factor, one, two)


def matern(left, right_x, right_y):
    diff_x = left[:, 0:1] - right_x
    diff_y = left[:, 1:2] - right_y
    t = SQRT_THREE * jnp.sqrt(diff_x * diff_x + diff_y * diff_y) / LENGTH_SCALE
    return (1.0 + t) * jnp.exp(-t)


def finish_kernel(first_ref, jitter_ref, keep_ref, recv_ref, own_ref, leadc_ref, leadr_ref, out_ref, work_ref):
    jitter = jitter_ref[0]
    lead_x, lead_y = leadr_ref[0:1, :], leadr_ref[1:2, :]
    share = PANEL // 2

    def eye(rows, first):
        row = lax.broadcasted_iota(jnp.int32, (rows, LEAD), 0) + first
        col = lax.broadcasted_iota(jnp.int32, (rows, LEAD), 1)
        return jnp.where(row == col, jitter, 0.0)

    block = matern(leadc_ref[...], lead_x, lead_y) + eye(LEAD, 0) - (keep_ref[PANEL:, :] + recv_ref[PANEL:, :])
    work_ref[:, :LEAD] = 0.5 * (block + block.T)
    diag = jnp.concatenate([eye(share, first_ref[0]), eye(share, first_ref[1])], axis=0)
    own = matern(own_ref[...], lead_x, lead_y) + diag - (keep_ref[:PANEL, :] + recv_ref[:PANEL, :])
    work_ref[:, LEAD:] = own.T

    rows = lax.broadcasted_iota(jnp.int32, (SUB, 1), 0)
    for top in range(0, LEAD, SUB):
        start = top // PANEL * PANEL
        part = work_ref[top : top + SUB, start:]
        for k in range(SUB):
            at = top + k - start
            column = part[:, at : at + 1]
            inv = lax.rsqrt(part[k : k + 1, at : at + 1])
            pivot = part[k : k + 1, :] * inv
            part = jnp.where(rows > k, part - (column * inv) * pivot, jnp.where(rows == k, pivot, part))
        work_ref[top : top + SUB, start:] = part
        low = top + SUB
        if low < LEAD:
            begin = low // PANEL * PANEL
            change = lax.dot_general(
                part[:, begin - start : LEAD - start], part[:, begin - start :], TT,
                precision=HIGHEST, preferred_element_type=jnp.float32,
            )
            work_ref[low:, begin:] -= change[low - begin :, :]
    out_ref[...] = work_ref[:, LEAD:].T


def finish(first, jitter, keep, recv, own, leadc, leadr):
    return pl.pallas_call(
        finish_kernel,
        in_specs=[smem(), smem(), vmem(), vmem(), vmem(), vmem(), vmem()],
        out_specs=vmem(),
        out_shape=jax.ShapeDtypeStruct((PANEL, LEAD), jnp.float32),
        scratch_shapes=[pltpu.VMEM((LEAD, LEAD + PANEL), jnp.float32)],
        name="finish",
    )(first, jitter, keep, recv, own, leadc, leadr)


def tail(factor, scales, coords, jitter, one, two):
    row_index = lax.axis_index("row")
    col_index = lax.axis_index("col")
    share = PANEL // 2
    begin = row_index * PANEL + col_index * share
    own = lax.dynamic_slice_in_dim(coords, begin, share, 2).reshape(2, PANEL)
    lead = coords[:, 0, :LEAD]
    first = jnp.stack([begin, begin + coords.shape[2]]).astype(jnp.int32)
    send, keep = partial_products(col_index[None].astype(jnp.int32), factor, scales[:, 0], one, two)
    recv = lax.ppermute(send, "col", [(0, 1), (1, 0)])
    out = finish(first, jitter, keep, recv, own.T, lead.T, lead)
    return out.reshape(2, share, LEAD)


def on_device(factor, scales, coords, jitter):
    row_index = lax.axis_index("row")
    own = dequantize_lead(factor, scales[:, 0])
    zero = jnp.zeros_like(own)
    one, two = lax.psum((jnp.where(row_index == 0, own, zero), jnp.where(row_index == 1, own, zero)), "row")
    return tail(factor, scales, coords, jitter, one, two)


def solution(mesh):
    placed = (P(None, "row", "col"), P(None, "row", "col"), P(), P())
    return jax.shard_map(
        on_device,
        mesh=mesh,
        in_specs=placed,
        out_specs=P(None, ("row", "col"), None),
        check_vma=False,
    )
```

time: 727 us -> 310 us (0.43)
  waiting for transfers between devices: 578 us -> 219 us
  other arithmetic: 80 us -> 10.1 us
  Pallas kernels: 0 us -> 59.3 us
  local copies, waits for them, and re-layouts: 37.9 us -> 4.98 us
  matrix products: 15.4 us -> 0 us
    psum x5 -> x1, waiting for transfers between devices: 578 us -> 219 us  [on_device(): lax.psum((jnp.where(row_index == 0, own, zero), jnp.where(row_index == 1,...]
    pallas_call x0 -> x3, Pallas kernels: none -> 59.3 us  [the longest x1 26 us: finish(): pl.pallas_call(finish_kernel, in_specs=[smem(), smem(), vmem(), vmem(), v...]
    another operation x10 -> x1, other arithmetic: 46.3 us -> 0.6 us  [tail(): first = jnp.stack([begin, begin + coords.shape[2]]).astype(jnp.int32)]
    convert_element_type x1 -> x0, other arithmetic: 23 us -> none  [on_device(): widened.astype(jnp.bfloat16).reshape(cycles * block_rows, width_local)]
    select_n x1 -> x0, local copies, waits for them, and re-layouts: 20.1 us -> none  [broadcast(): return lax.psum(jnp.where(mine, value, jnp.zeros_like(value)), axis)]
    dot_general x2 -> x0, matrix products: 14.7 us -> none  [the longest x1 13.6 us: on_device(): lax.dot_general(dequant, leading, (((1,), (1,)), ((), ())), preferred_ele...]
    unnamed x2 -> x6, local copies, waits for them, and re-layouts: 10.7 us -> 2.01 us
  transfers between devices with their start and end apart: 5 -> 2, of which waited for: 5 -> 1; matrix products, arithmetic and copies ran while one was open for 4% -> 1% of each run, Pallas kernels for 0% -> 0%
where the time goes in v1:
time: 310 us; the launch traced here: 308 us
  waiting for transfers between devices  219 us (71%)
  Pallas kernels  59.3 us (19%)
  between operations  14.1 us (5%)
  other arithmetic  10.1 us (3%)
  local copies, waits for them, and re-layouts  4.98 us (2%)
    psum x1, waiting for transfers between devices, on_device(): lax.psum((jnp.where(row_index == 0, own, zero), jnp.where(row_index == 1,...  219 us
    pallas_call x1, Pallas kernels, finish(): pl.pallas_call(finish_kernel, in_specs=[smem(), smem(), vmem(), vmem(), v...  26 us
    pallas_call x1, Pallas kernels, partial_products(): pl.pallas_call(products_kernel, grid=(width // STEP,), in_specs=[smem(),...  21 us
    pallas_call x1, Pallas kernels, dequantize_lead(): pl.pallas_call(dequant_kernel, grid=(width // STEP,), in_specs=[smem(), p...  12.3 us
    select_n x1, other arithmetic, on_device(): jnp.where(row_index == 1, own, zero)  9.5 us
  transfers between devices with their start and end apart: 2, of which 1 were waited for; matrix products, arithmetic and copies ran while one was open for 1% of the time, Pallas kernels for 0%

profile of v1, /device:TPU:0, one launch (start us, length us, event | category | flops | bytes accessed | tf_op | source)
XLA Modules:
  0.0 307.8 jit_solution(15022389613108492598)
XLA Ops:
  6.5 0.0 all-reduce.3.cloned.1.call-start
  6.5 1.3 copy.13
  7.8 12.3 %dequantize_lead.1 = bf16[128,32768]{1,0:T(8,128)(2,1)} custom-call(f32[2,256]{1,0:T(2,128)} %bitcast.17, bf16[2,128,32768]{2,1,0:T(8,128)(2,1)} %factor_ref.3), custom_call_target="tpu_custom_call" | custom-call | tf_op jit(solution)/shard_map/dequantize_lead/pallas_call | solution.py:43
  20.1 9.5 %broadcast_select_fusion = (bf16[128,32768]{1,0:T(8,128)(2,1)}, bf16[128,32768]{1,0:T(8,128)(2,1)}) fusion(bf16[128,32768]{1,0:T(8,128)(2,1)} %dequantize_lead.1, pred[]{:T(512)S(6)} %eq.7, pred[]{:T(512)S(6)} %eq.6), kind=kLoop, calls=%fused_computation | loop fusion | flops 8388608 | bytes 25165826 | tf_op jit(solution)/shard_map/jit(_where)/select_n | solution.py:174
  29.6 0.0 all-reduce.3.cloned.1.call-update
  29.7 219.4 %all-reduce.3.cloned.1.call-done = (bf16[128,32768]{1,0:T(8,128)(2,1)}, bf16[128,32768]{1,0:T(8,128)(2,1)}) async-done(((bf16[128,32768]{1,0:T(8,128)(2,1)}, bf16[128,32768]{1,0:T(8,128)(2,1)}), (bf16[128,32768]{1,0:T(8,128)(2,1)}, bf16[128,32768]{1,0:T(8,128)(2,1)})) %all-reduce.3.cloned.1.call-update) | async-done | bytes 16777232 | tf_op jit(solution)/shard_map/psum | solution.py:174
  249.1 21.0 %partial_products.1 = (f32[384,256]{1,0:T(8,128)}, f32[384,256]{1,0:T(8,128)}) custom-call(s32[1]{0:T(128)} %bitcast.2.col_ref, f32[2,256]{1,0:T(2,128)} %bitcast.18, bf16[2,128,32768]{2,1,0:T(8,128)(2,1)} %factor_ref.3, bf16[128,32768]{1,0:T(8,128)(2,1)} %get-tuple-element.9.one_ref, bf16[128,32768]{1,0:T(8,128)(2,1)} %get-tuple-element.10.two_ref), custom_call_target="tpu_custom_call" | custom-call | tf_op jit(solution)/shard_map/partial_products/pallas_call | solution.py:83
  270.0 0.0 collective-permute-start
  270.0 0.7 slice.3
  270.7 0.8 constant_dynamic-slice_fusion
  271.5 0.7 copy.5
  272.2 0.0 copy-start.1
  272.2 0.8 copy.7.leadc_ref
  273.7 0.6 pad_add_fusion.first_ref
  274.3 0.0 collective-permute-done.recv_ref
  274.3 0.0 copy-start
  274.3 0.0 copy-done.1
  274.3 0.7 copy-done
  275.0 26.0 %finish.1 = f32[128,256]{1,0:T(8,128)} custom-call(s32[2]{0:T(128)} %pad_add_fusion.first_ref, f32[1]{0:T(128)S(6)} %copy.17.jitter_ref, f32[384,256]{1,0:T(8,128)} %get-tuple-element.7.keep_ref, f32[384,256]{1,0:T(8,128)} %copy-done, f32[128,2]{1,0:T(8,128)} %bitcast.16, f32[256,2]{1,0:T(8,128)} %copy.7.leadc_ref, f32[2,256]{1,0:T(2,128)} %bitcast.20), custom_call_target="tpu_custom_call" | custom-call | tf_op jit(solution)/shard_map/finish/pallas_call | solution.py:146
  (1 shorter events, 0.0 us)
Async XLA Ops:
  6.5 242.5 %all-reduce.3.cloned.1.call-start = ((), (), s32[]{:S(2)}) async-start(), calls=%async_computation | async-start | bytes 33554432 | tf_op jit(solution)/shard_map/psum | solution.py:174
  270.0 4.2 %collective-permute-start = (f32[384,256]{1,0:T(8,128)}, f32[384,256]{1,0:T(8,128)S(1)}, u32[]{:S(2)}, u32[]{:S(2)}) collective-permute-start(f32[384,256]{1,0:T(8,128)} %get-tuple-element.8), channel_id=1, source_target_pairs={{0,1},{1,0},{2,3},{3,2},{4,5},{5,4},{6,7},{7,6},{8,9},{9,8},{10,11... | collective-permute-start | bytes 1179656 | tf_op jit(solution)/shard_map/ppermute | solution.py:165
  272.2 2.1 copy-start.1
  274.3 0.7 copy-start
Sparse Core Ops, SparseCore 0:
  29.8 219.2 all-reduce.2
